TPU v7x, 32 devices: a whole 2x2x4 slice. The times are simulated.
32 devices in a mesh: wide: 8 (over z, x), grp: 4 (over y, core).
Axes of the slice: x: 2, y: 2, z: 4, core: 2. Of those that a mesh axis runs over, the one named last changes fastest.
Arguments:
- query_rows: bfloat16 [4096, 1280], P(('wide', 'grp')), may hold values from -9 to 9, as said below
- key_rows: bfloat16 [4096, 1280], P(('wide', 'grp')), may hold values from -9 to 9, as said below
- value_rows: bfloat16 [4096, 1280], P(('wide', 'grp')), may hold values from -6 to 6
- block_image: int32 [32], replicated, may hold values from 0 to 6, never falling along the last dimension, each value on 1 to 8 neighbouring positions
Outputs:
- attended: bfloat16 [4096, 1280], P(('wide', 'grp'))
Inputs may be any that keep to these rules, and one draw needn't show every extreme that they name: `query_rows`: Queries: entries bounded as stated. `key_rows`: Keys: entries bounded as stated. `block_image`: image numbers never fall along the window; every image covers 1 to 8 whole blocks and one covers exactly 8.
All inputs are finite; a program needn't handle non-finite values.
Results may differ from a plain program's by a relative error of at most 0.004.
Values may be sent and summed in bfloat16 or wider, within the bound.
A program may use at most 64 MiB of HBM per device.

v0:
```python
import functools
import math

import jax
import jax.numpy as jnp
from jax import lax
from jax.experimental import pallas as pl
from jax.experimental.pallas import tpu as pltpu
from jax.sharding import PartitionSpec as P

HDIM = 80
BLK = 128
MOST = 8
NEG = -1e30
EARLY = 4
MESH = pl.DeviceIdType.MESH


def kernel(cfg, img, q_hbm, k_hbm, v_hbm, out, q_in, k_in, v_in, k_src, q_src, v_src, k_own, q_own, v_own,
           k_halo, v_halo, kn_own, kn_halo, m_scr, l_scr, acc, s_scr, p_near, p_far, o_src, o_own,
           k_ss, k_rs, q_ss, q_rs, v_ss, v_rs, k_up, k_dn, k_hr, v_up, v_dn, v_hr, o_ss, o_rs, loc_s):
    planes, fold, grp, heads = cfg
    n = fold * grp
    cols = heads * HDIM
    wide_at, grp_at = lax.axis_index("wide"), lax.axis_index("grp")
    plane = wide_at // fold
    fold_at = wide_at % fold
    me = fold_at * grp + grp_at
    has_prev, has_next = plane > 0, plane < planes - 1

    loads = [pltpu.make_async_copy(src, dst, loc_s.at[i])
             for i, (src, dst) in enumerate(((k_hbm, k_in), (q_hbm, q_in), (v_hbm, v_in)))]
    for load in loads:
        load.start()

    def device(at_plane, member):
        return (at_plane * fold + member // grp, member % grp)

    def turn_of(j):
        return j % 2 * (n // 2 + j // 2) + (1 - j % 2) * (j // 2)

    def to_peer(j):
        i = turn_of(j)
        return ((fold_at + i // grp) % fold) * grp + (grp_at + i % grp) % grp

    def from_peer(j):
        i = turn_of(j)
        return ((fold_at + fold - i // grp) % fold) * grp + (grp_at + grp - i % grp) % grp

    barrier = pltpu.get_barrier_semaphore()
    for i in range(1, n):
        pl.semaphore_signal(barrier, inc=1, device_id=device(plane, to_peer(i)), device_id_type=MESH)

    @pl.when(has_prev)
    def _():
        pl.semaphore_signal(barrier, inc=1, device_id=device(plane - 1, me), device_id_type=MESH)

    @pl.when(has_next)
    def _():
        pl.semaphore_signal(barrier, inc=1, device_id=device(plane + 1, me), device_id_type=MESH)

    def turn(ref, dst):
        whole = jnp.concatenate([ref[:, c:c + BLK].T for c in range(0, n * cols, BLK)], axis=0)
        for member in range(n):
            dst[member] = whole[member * cols:(member + 1) * cols]

    @pl.when(jnp.logical_not(has_prev))
    def _():
        for ref in (k_halo, v_halo):
            ref[0:n] = jnp.zeros((n,) + ref.shape[1:], ref.dtype)

    @pl.when(jnp.logical_not(has_next))
    def _():
        for ref in (k_halo, v_halo):
            ref[n:2 * n] = jnp.zeros((n,) + ref.shape[1:], ref.dtype)

    for load, ref, dst in zip(loads, (k_in, q_in, v_in), (k_src, q_src, v_src)):
        load.wait()
        turn(ref, dst)

    pl.semaphore_wait(barrier, n - 1 + has_prev.astype(jnp.int32) + has_next.astype(jnp.int32))

    def remote(src, dst, ss, rs, dev):
        return pltpu.make_async_remote_copy(src_ref=src, dst_ref=dst, send_sem=ss, recv_sem=rs,
                                            device_id=dev, device_id_type=MESH)

    k_halos, v_halos = (k_halo, k_up, k_dn, k_hr), (v_halo, v_up, v_dn, v_hr)

    def up(halos, member, src):
        halo, ss, _, rs = halos
        return remote(src, halo.at[member], ss.at[member], rs.at[member], device(plane + 1, me))

    def down(halos, member, src):
        halo, _, ss, rs = halos
        return remote(src, halo.at[n + member], ss.at[member], rs.at[n + member], device(plane - 1, me))

    def forward(halos, member, src):
        @pl.when(jnp.logical_and(has_next, member >= 1))
        def _():
            up(halos, member, src).start()

        @pl.when(jnp.logical_and(has_prev, member <= n - 2))
        def _():
            down(halos, member, src).start()

    def k_copy(src, dst):
        return remote(k_src.at[dst], k_own.at[src], k_ss.at[dst], k_rs.at[src], device(plane, dst))

    def q_copy(src, dst):
        return remote(q_src.at[dst], q_own.at[src], q_ss.at[dst], q_rs.at[src], device(plane, dst))

    def v_copy(src, dst):
        return remote(v_src.at[dst], v_own.at[src], v_ss.at[dst], v_rs.at[src], device(plane, dst))

    forward(k_halos, me, k_src.at[me])
    for i in range(1, n):
        k_copy(me, to_peer(i)).start()
    for i in range(1, EARLY + 1):
        v_copy(me, to_peer(i)).start()
    q_copy(me, me // 2 * 2 + 1 - me % 2).start()
    for step in range(1, n // 2):
        for r in range(2):
            q_copy(me, (me // 2 + n // 2 - step) % (n // 2) * 2 + r).start()
    for i in range(EARLY + 1, n):
        v_copy(me, to_peer(i)).start()
    forward(v_halos, me, v_src.at[me])
    keeps = [pltpu.make_async_copy(src.at[me], dst.at[me], loc_s.at[i])
             for i, (src, dst) in enumerate(((k_src, k_own), (q_src, q_own), (v_src, v_own)))]
    for keep in keeps:
        keep.start()

    def natural(src, dst):
        for h in range(heads):
            dst[h] = src[h * HDIM:(h + 1) * HDIM].T

    keeps[0].wait()
    natural(k_own.at[me], kn_own.at[me])

    def take_k(i, carry):
        source = from_peer(i)
        k_copy(source, me).wait_recv()
        forward(k_halos, source, k_own.at[source])
        natural(k_own.at[source], kn_own.at[source])
        return carry

    lax.fori_loop(1, n, take_k, 0)
    for keep in keeps[1:]:
        keep.wait()
    def take_v(i):
        source = from_peer(i)
        v_copy(source, me).wait_recv()
        forward(v_halos, source, v_own.at[source])

    for i in range(1, EARLY + 1):
        take_v(i)
    factor = math.log2(math.e) / math.sqrt(HDIM)
    blocks = img.shape[0]
    lane = lax.broadcasted_iota(jnp.int32, (1, 2 * BLK), 1)
    base = plane * n
    pairs = n // 2

    def live_row(first, key_block):
        inside = jnp.logical_and(key_block >= 0, key_block < blocks)
        key_id = img[jnp.clip(key_block, 0, blocks - 1)]
        key_id = jnp.where(inside, key_id, -2)
        ids = jnp.where(lane < BLK, img[first], img[first + 1])
        return ids == key_id

    def weights(h, pair, keys, live, start, p_dst):
        q_pair = jnp.concatenate([q_own[2 * pair, pl.ds(h * HDIM, HDIM)],
                                  q_own[2 * pair + 1, pl.ds(h * HDIM, HDIM)]], axis=1)
        top = start
        for t in range(n):
            s = jnp.dot(keys(t), q_pair, preferred_element_type=jnp.float32)
            s_scr[h, t] = s
            top = jnp.maximum(top, jnp.where(live[t], jnp.max(s, axis=0, keepdims=True), NEG))
        total = jnp.zeros((8, 2 * BLK), jnp.float32)
        for t in range(n):
            shift = jnp.where(live[t], -top * factor, NEG)
            w = jnp.exp2(s_scr[h, t] * factor + shift)
            total = total + jnp.sum(w.reshape(BLK // 8, 8, 2 * BLK), axis=0)
            p_dst[t * BLK:(t + 1) * BLK] = w.astype(jnp.bfloat16)
        return top, jnp.sum(total, axis=0, keepdims=True)

    def times(values, p_src):
        v = jnp.concatenate([values(t) for t in range(n)], axis=1)
        return jnp.dot(v, p_src[...], preferred_element_type=jnp.float32)

    def near(step, carry):
        pair = (me // 2 + step) % pairs
        for r in range(2):
            @pl.when(2 * pair + r != me)
            def _():
                q_copy(2 * pair + r, me).wait_recv()
        first = base + 2 * pair
        live = [live_row(first, base + t) for t in range(n)]
        for h in range(heads):
            at = pair * heads + h
            m_scr[at], l_scr[at] = weights(h, pair, lambda t: kn_own[t, h], live,
                                           jnp.full((1, 2 * BLK), NEG, jnp.float32), p_near.at[at])
        return carry

    lax.fori_loop(0, pairs, near, 0)

    def take_halo(halos, src):
        @pl.when(has_prev)
        def _():
            for member in range(1, n):
                up(halos, member, src.at[member]).wait_recv()

        @pl.when(has_next)
        def _():
            for member in range(n - 1):
                down(halos, member, src.at[member]).wait_recv()

    take_halo(k_halos, k_own)

    def turn_halo(slot, carry):
        natural(k_halo.at[slot], kn_halo.at[slot])
        return carry

    cuts = [1 + (2 * n - 2) * i // (n - 1 - EARLY) for i in range(n - EARLY)]
    for i in range(EARLY + 1, n):
        take_v(i)
        lax.fori_loop(cuts[i - EARLY - 1], cuts[i - EARLY], turn_halo, 0)

    def far(pair, carry):
        first = base + 2 * pair
        live = []
        for t in range(n):
            slot = 2 * pair + 1 + t
            live.append(live_row(first, jnp.where(slot < n, base - n + slot, base + slot)))
        for h in range(heads):
            at = pair * heads + h
            top1 = m_scr[at]
            top, total = weights(h, pair, lambda t: kn_halo[2 * pair + 1 + t, h], live, top1, p_far.at[at])
            fade = jnp.exp2((top1 - top) * factor)
            out_t = times(lambda t: v_own[t, h * HDIM:(h + 1) * HDIM], p_near.at[at])
            acc[at] = out_t * fade
            l_scr[at] = l_scr[at] * fade + total
        return carry

    lax.fori_loop(0, pairs, far, 0)
    take_halo(v_halos, v_own)

    def out_copy(src, dst):
        return remote(o_src.at[dst], o_own.at[src], o_ss.at[dst], o_rs.at[src], device(plane, dst))

    def finish(step, carry):
        pair = (me // 2 + 1 + step) % pairs
        for h in range(heads):
            at = pair * heads + h
            out_t = times(lambda t: v_halo[2 * pair + 1 + t, h * HDIM:(h + 1) * HDIM], p_far.at[at])
            res = ((acc[at] + out_t) / l_scr[at]).astype(jnp.bfloat16)
            o_src[2 * pair, h * HDIM:(h + 1) * HDIM] = res[:, :BLK]
            o_src[2 * pair + 1, h * HDIM:(h + 1) * HDIM] = res[:, BLK:]
        for r in range(2):
            dst = 2 * pair + r

            @pl.when(dst != me)
            def _():
                out_copy(me, dst).start()

            @pl.when(dst == me)
            def _():
                pltpu.make_async_copy(o_src.at[me], o_own.at[me], loc_s.at[0]).start()
        return carry

    lax.fori_loop(0, pairs, finish, 0)

    pltpu.make_async_copy(o_src.at[me], o_own.at[me], loc_s.at[0]).wait()
    for i in range(1, n):
        out_copy(from_peer(i), me).wait_recv()
    flat = jnp.concatenate([o_own[member] for member in range(n)], axis=0)
    for c in range(0, n * cols, BLK):
        out[:, c:c + BLK] = flat[c:c + BLK].T

    for copy in (k_copy, q_copy, v_copy, out_copy):
        for i in range(1, n):
            copy(me, to_peer(i)).wait_send()

    for halos, src in ((k_halos, k_own), (v_halos, v_own)):
        @pl.when(has_next)
        def _():
            for member in range(1, n):
                up(halos, member, src.at[member]).wait_send()

        @pl.when(has_prev)
        def _():
            for member in range(n - 1):
                down(halos, member, src.at[member]).wait_send()


def solution(mesh):
    wide, grp = mesh.shape["wide"], mesh.shape["grp"]
    fold = MOST // grp
    n = fold * grp
    planes = wide // fold

    def body(query_rows, key_rows, value_rows, block_image):
        rows, width = query_rows.shape
        heads = width // HDIM // n
        cols = heads * HDIM
        bf, f32 = jnp.bfloat16, jnp.float32
        vmem = pl.BlockSpec(memory_space=pltpu.VMEM)
        hbm = pl.BlockSpec(memory_space=pl.ANY)
        dma = pltpu.SemaphoreType.DMA
        units = n // 2 * heads
        slices = pltpu.VMEM((n, cols, BLK), bf)
        return pl.pallas_call(
            functools.partial(kernel, (planes, fold, grp, heads)),
            out_shape=jax.ShapeDtypeStruct((rows, width), bf),
            in_specs=[pl.BlockSpec(memory_space=pltpu.SMEM), hbm, hbm, hbm],
            out_specs=vmem,
            scratch_shapes=[pltpu.VMEM((rows, width), bf)] * 3 + [slices] * 6 + [
                pltpu.VMEM((2 * n, cols, BLK), bf),
                pltpu.VMEM((2 * n, cols, BLK), bf),
                pltpu.VMEM((n, heads, BLK, HDIM), bf),
                pltpu.VMEM((2 * n, heads, BLK, HDIM), bf),
                pltpu.VMEM((units, 1, 2 * BLK), f32),
                pltpu.VMEM((units, 1, 2 * BLK), f32),
                pltpu.VMEM((units, HDIM, 2 * BLK), f32),
                pltpu.VMEM((heads, n, BLK, 2 * BLK), f32),
                pltpu.VMEM((units, n * BLK, 2 * BLK), bf),
                pltpu.VMEM((units, n * BLK, 2 * BLK), bf),
                slices, slices,
            ] + [dma((n,))] * 6 + [dma((n,)), dma((n,)), dma((2 * n,))] * 2 + [dma((n,)), dma((n,)), dma((3,))],
            compiler_params=pltpu.CompilerParams(collective_id=0, has_side_effects=True),
        )(block_image, query_rows, key_rows, value_rows)

    return jax.shard_map(
        body,
        mesh=mesh,
        in_specs=(
            P(("wide", "grp"), None),
            P(("wide", "grp"), None),
            P(("wide", "grp"), None),
            P(),
        ),
        out_specs=P(("wide", "grp"), None),
        check_vma=False,
    )
```

profile of v0, /device:TPU:0, one launch (start us, length us, event | category | flops | bytes accessed | tf_op | source)
XLA Modules:
  0.0 30.8 jit_solution(7882767889536057410)
XLA Ops:
  0.0 29.1 %shard_map.46 = bf16[128,1280]{1,0:T(8,128)(2,1)} custom-call(s32[32]{0:T(128)} %img.1, bf16[128,1280]{1,0:T(8,128)(2,1)} %q_hbm.1, bf16[128,1280]{1,0:T(8,128)(2,1)} %k_hbm.1, bf16[128,1280]{1,0:T(8,128)(2,1)} %v_hbm.1), custom_call_target="tpu_custom_call" | custom-call | tf_op jit(solution)/shard_map/pallas_call | solution.py:310
  29.1 1.7 %copy.6 = bf16[128,1280]{1,0:T(8,128)(2,1)} copy(bf16[128,1280]{1,0:T(8,128)(2,1)} %shard_map.46) | data formatting | bytes 655360
where the time goes:
time: 31.1 us; the launch traced here: 30.8 us
  Pallas kernels  29.1 us (94%)
  local copies, waits for them, and re-layouts  1.72 us (6%)
    pallas_call x1, Pallas kernels, body(): pl.pallas_call(functools.partial(kernel, (planes, fold, grp, heads)), out...  29.1 us
    unnamed x1, local copies, waits for them, and re-layouts  1.72 us

commit v1 on v0

v1 whole, which is shorter than its diff:
```python
import functools
import math

import jax
import jax.numpy as jnp
from jax import lax
from jax.experimental import pallas as pl
from jax.experimental.pallas import tpu as pltpu
from jax.sharding import PartitionSpec as P

HDIM = 80
BLK = 128
MOST = 8
NEG = -1e30
MESH = pl.DeviceIdType.MESH


def kernel(cfg, img_hbm, q_hbm, k_hbm, v_hbm, out, img, q_in, k_in, v_in, k_src, q_src, v_src,
           k_own, q_own, v_own, k_halo, v_halo, kn, vt, l_scr, s_scr, p_scr, o_src, o_own,
           load_s, k_rs, q_rs, v_rs, o_rs, send_s, halo_ss, halo_rs, keep_s):
    planes, fold, grp, heads = cfg
    n = fold * grp
    cols = heads * HDIM
    pairs = n // 2
    wide_at, grp_at = lax.axis_index("wide"), lax.axis_index("grp")
    plane = wide_at // fold
    fold_at = wide_at % fold
    me = fold_at * grp + grp_at
    mine = me // 2
    mate = mine * 2 + 1 - me % 2
    has_prev, has_next = plane > 0, plane < planes - 1

    loads = [pltpu.make_async_copy(src, dst, load_s.at[i])
             for i, (src, dst) in enumerate(((k_hbm, k_in), (q_hbm, q_in), (v_hbm, v_in), (img_hbm, img)))]
    for load in loads:
        load.start()
    def device(at_plane, member):
        return (at_plane * fold + member // grp, member % grp)

    barrier = pltpu.get_barrier_semaphore()
    for i in range(1, n):
        pl.semaphore_signal(barrier, inc=1, device_id=device(plane, (me + i) % n), device_id_type=MESH)

    @pl.when(has_prev)
    def _():
        pl.semaphore_signal(barrier, inc=1, device_id=device(plane - 1, me), device_id_type=MESH)

    @pl.when(has_next)
    def _():
        pl.semaphore_signal(barrier, inc=1, device_id=device(plane + 1, me), device_id_type=MESH)

    @pl.when(jnp.logical_not(has_prev))
    def _():
        for ref in (kn, vt):
            ref[0:n - 1] = jnp.zeros((n - 1,) + ref.shape[1:], ref.dtype)

    @pl.when(jnp.logical_not(has_next))
    def _():
        for ref in (kn, vt):
            ref[2 * n - 1:3 * n - 2] = jnp.zeros((n - 1,) + ref.shape[1:], ref.dtype)
    def turn(ref, dst):
        whole = jnp.concatenate([ref[:, c:c + BLK].T for c in range(0, n * cols, BLK)], axis=0)
        for member in range(n):
            dst[member] = whole[member * cols:(member + 1) * cols]

    def remote(src, dst, ss, rs, dev):
        return pltpu.make_async_remote_copy(src_ref=src, dst_ref=dst, send_sem=ss, recv_sem=rs,
                                            device_id=dev, device_id_type=MESH)

    def exchange(src, dst, ss, rs):
        def send(to):
            remote(src.at[to], dst.at[me], ss, rs.at[mine], device(plane, to)).start()

        def take(pair):
            remote(src.at[pl.ds(0, 2)], dst.at[pl.ds(2 * pair, 2)], ss, rs.at[pair], device(plane, mate)).wait_recv()

        def take_mate():
            remote(src.at[0], dst.at[mate], ss, rs.at[mine], device(plane, mate)).wait_recv()

        def sent():
            part = src.at[pl.ds(0, n - 1)]
            remote(part, part, ss, rs.at[0], device(plane, mate)).wait_send()
        return send, take, take_mate, sent

    k_send, k_take, k_mate, k_sent = exchange(k_src, k_own, send_s.at[0], k_rs)
    q_send, q_take, q_mate, q_sent = exchange(q_src, q_own, send_s.at[1], q_rs)
    v_send, v_take, v_mate, v_sent = exchange(v_src, v_own, send_s.at[2], v_rs)

    def forward(which, halo, member, src):
        @pl.when(jnp.logical_and(has_next, member >= 1))
        def _():
            remote(src, halo.at[member - 1], halo_ss.at[which, 0], halo_rs.at[which, 0],
                   device(plane + 1, me)).start()

        @pl.when(jnp.logical_and(has_prev, member <= n - 2))
        def _():
            remote(src, halo.at[n - 1 + member], halo_ss.at[which, 1], halo_rs.at[which, 1],
                   device(plane - 1, me)).start()

    def take_below(which, halo):
        part = halo.at[pl.ds(0, n - 1)]
        remote(part, part, halo_ss.at[which, 0], halo_rs.at[which, 0], device(plane, mate)).wait_recv()

    def take_above(which, halo):
        part = halo.at[pl.ds(n - 1, n - 1)]
        remote(part, part, halo_ss.at[which, 1], halo_rs.at[which, 1], device(plane, mate)).wait_recv()

    def sent_up(which, halo):
        part = halo.at[pl.ds(0, n - 1)]
        remote(part, part, halo_ss.at[which, 0], halo_rs.at[which, 0], device(plane, mate)).wait_send()

    def sent_down(which, halo):
        part = halo.at[pl.ds(n - 1, n - 1)]
        remote(part, part, halo_ss.at[which, 1], halo_rs.at[which, 1], device(plane, mate)).wait_send()

    def out_order(send):
        for step in range(1, pairs):
            for r in range(2):
                send((mine + pairs - step) % pairs * 2 + r)

    loads[0].wait()
    turn(k_in, k_src)
    pl.semaphore_wait(barrier, n - 1 + has_prev.astype(jnp.int32) + has_next.astype(jnp.int32))
    forward(0, k_halo, me, k_src.at[me])
    k_send(mate)
    out_order(k_send)
    loads[2].wait()
    turn(v_in, v_src)
    forward(1, v_halo, me, v_src.at[me])
    v_send(mate)
    loads[1].wait()
    turn(q_in, q_src)
    q_send(mate)
    out_order(v_send)
    out_order(q_send)
    keep = pltpu.make_async_copy(q_src.at[me], q_own.at[me], keep_s.at[0])
    keep.start()
    def natural(slot, src):
        kn[slot] = src[...].T

    natural(n - 1 + me, k_src.at[me])
    vt[n - 1 + me] = v_src[me]
    k_mate()
    forward(0, k_halo, mate, k_own.at[mate])
    natural(n - 1 + mate, k_own.at[mate])
    def take_k(step, carry):
        pair = (mine + step) % pairs
        k_take(pair)
        for r in range(2):
            forward(0, k_halo, 2 * pair + r, k_own.at[2 * pair + r])
        for r in range(2):
            natural(n - 1 + 2 * pair + r, k_own.at[2 * pair + r])
        return carry

    lax.fori_loop(1, pairs, take_k, 0)
    v_mate()
    forward(1, v_halo, mate, v_own.at[mate])
    vt[n - 1 + mate] = v_own[mate]
    def take_v(step, carry):
        pair = (mine + step) % pairs
        v_take(pair)
        for r in range(2):
            forward(1, v_halo, 2 * pair + r, v_own.at[2 * pair + r])
        for r in range(2):
            vt[n - 1 + 2 * pair + r] = v_own[2 * pair + r]
        return carry

    lax.fori_loop(1, pairs, take_v, 0)
    def turn_below(i, carry):
        natural(i, k_halo.at[i])
        return carry

    def turn_above(i, carry):
        natural(n + i, k_halo.at[i])
        return carry

    @pl.when(has_prev)
    def _():
        take_below(0, k_halo)
        lax.fori_loop(0, n - 1, turn_below, 0)

    @pl.when(has_next)
    def _():
        take_above(0, k_halo)
        lax.fori_loop(n - 1, 2 * n - 2, turn_above, 0)
    loads[3].wait()
    factor = math.log2(math.e) / math.sqrt(HDIM)
    blocks = img.shape[0]
    base = plane * n

    def span(block):
        own_id = img[block]
        before, after = jnp.int32(0), jnp.int32(0)
        for d in range(1, MOST):
            low = jnp.where(block >= d, img[jnp.maximum(block - d, 0)], -1)
            high = jnp.where(block + d < blocks, img[jnp.minimum(block + d, blocks - 1)], -1)
            before += (low == own_id).astype(jnp.int32)
            after += (high == own_id).astype(jnp.int32)
        return before, before + after + 1

    def first_slot(m):
        before, count = span(base + m)
        return m + n - 1 - before, count

    def weights(m, slot):
        start, count = first_slot(m)
        rows = []
        for h in range(heads):
            q_h = q_own[m, h * HDIM:(h + 1) * HDIM]
            none = jnp.zeros_like(q_h)
            rows.append(jnp.concatenate([q_h if j == h else none for j in range(heads)], axis=1))
        q_all = jnp.concatenate(rows, axis=0)
        top = jnp.full((1, heads * BLK), NEG, jnp.float32)
        for t in range(MOST):
            s = jnp.dot(kn[start + t], q_all, preferred_element_type=jnp.float32)
            s_scr[slot, t] = s
            top = jnp.maximum(top, jnp.where(t < count, jnp.max(s, axis=0, keepdims=True), NEG))
        total = jnp.zeros((8, heads * BLK), jnp.float32)
        for t in range(MOST):
            shift = jnp.where(t < count, -top * factor, NEG)
            w = jnp.exp2(s_scr[slot, t] * factor + shift)
            total = total + jnp.sum(w.reshape(BLK // 8, 8, heads * BLK), axis=0)
            p_scr[m, t * BLK:(t + 1) * BLK] = w.astype(jnp.bfloat16)
        l_scr[m] = jnp.sum(total, axis=0, keepdims=True)

    def score(pair):
        for r in range(2):
            weights(2 * pair + r, r)

    def score_step(step, carry):
        pair = (mine + step) % pairs
        @pl.when(step == 0)
        def _():
            keep.wait()
            q_mate()
        @pl.when(step > 0)
        def _():
            q_take(pair)
        score(pair)
        return carry

    lax.fori_loop(0, pairs, score_step, 0)
    def move_below(i, carry):
        vt[i] = v_halo[i]
        return carry

    def move_above(i, carry):
        vt[n + i] = v_halo[i]
        return carry

    @pl.when(has_prev)
    def _():
        take_below(1, v_halo)
        lax.fori_loop(0, n - 1, move_below, 0)

    @pl.when(has_next)
    def _():
        take_above(1, v_halo)
        lax.fori_loop(n - 1, 2 * n - 2, move_above, 0)
    o_send, o_take, o_mate, o_sent = exchange(o_src, o_own, send_s.at[3], o_rs)

    def finish(step, carry):
        pair = (mine + 1 + step) % pairs
        for r in range(2):
            m = 2 * pair + r
            start, _ = first_slot(m)
            v = jnp.concatenate([vt[start + t] for t in range(MOST)], axis=1)
            res = jnp.dot(v, p_scr[m], preferred_element_type=jnp.float32)
            res = jnp.concatenate([res[h * HDIM:(h + 1) * HDIM, h * BLK:(h + 1) * BLK]
                                   / l_scr[m, :, h * BLK:(h + 1) * BLK] for h in range(heads)], axis=0)
            o_src[m] = res.astype(jnp.bfloat16)
        for r in range(2):
            m = 2 * pair + r

            @pl.when(m != me)
            def _():
                o_send(m)
        return carry

    lax.fori_loop(0, pairs, finish, 0)
    o_own[me] = o_src[me]
    k_sent()
    q_sent()
    v_sent()
    for which, halo in ((0, k_halo), (1, v_halo)):
        @pl.when(has_next)
        def _():
            sent_up(which, halo)

        @pl.when(has_prev)
        def _():
            sent_down(which, halo)
    o_mate()
    for step in range(1, pairs):
        o_take((mine + step) % pairs)
    flat = jnp.concatenate([o_own[member] for member in range(n)], axis=0)
    for c in range(0, n * cols, BLK):
        out[:, c:c + BLK] = flat[c:c + BLK].T
    o_sent()


def solution(mesh):
    wide, grp = mesh.shape["wide"], mesh.shape["grp"]
    fold = MOST // grp
    n = fold * grp
    planes = wide // fold

    def body(query_rows, key_rows, value_rows, block_image):
        rows, width = query_rows.shape
        heads = width // HDIM // n
        cols = heads * HDIM
        bf, f32 = jnp.bfloat16, jnp.float32
        hbm = pl.BlockSpec(memory_space=pltpu.HBM)
        dma = pltpu.SemaphoreType.DMA
        slices = pltpu.VMEM((n, cols, BLK), bf)
        halo = pltpu.VMEM((2 * n - 2, cols, BLK), bf)
        lanes = heads * BLK
        args = [pltpu.with_memory_space_constraint(a, pltpu.HBM)
                for a in (block_image, query_rows, key_rows, value_rows)]
        return pl.pallas_call(
            functools.partial(kernel, (planes, fold, grp, heads)),
            out_shape=jax.ShapeDtypeStruct((rows, width), bf),
            in_specs=[hbm] * 4,
            out_specs=pl.BlockSpec(memory_space=pltpu.VMEM),
            scratch_shapes=[pltpu.SMEM(block_image.shape, jnp.int32)]
            + [pltpu.VMEM((rows, width), bf)] * 3 + [slices] * 6 + [halo] * 2 + [
                pltpu.VMEM((3 * n - 2, BLK, cols), bf),
                pltpu.VMEM((3 * n - 2, cols, BLK), bf),
                pltpu.VMEM((n, 1, lanes), f32),
                pltpu.VMEM((2, MOST, BLK, lanes), f32),
                pltpu.VMEM((n, MOST * BLK, lanes), bf),
                slices, slices,
            ] + [dma((4,))] + [dma((n // 2,))] * 4 + [dma((4,)), dma((2, 2)), dma((2, 2)), dma((1,))],
            compiler_params=pltpu.CompilerParams(collective_id=0, has_side_effects=True,
                                                 vmem_limit_bytes=40 << 20),
        )(*args)

    return jax.shard_map(
        body,
        mesh=mesh,
        in_specs=(
            P(("wide", "grp"), None),
            P(("wide", "grp"), None),
            P(("wide", "grp"), None),
            P(),
        ),
        out_specs=P(("wide", "grp"), None),
        check_vma=False,
    )
```

time: 31.1 us -> 27.5 us (0.88)
  Pallas kernels: 29.1 us -> 26.5 us
  local copies, waits for them, and re-layouts: 1.72 us -> 0.73 us
    pallas_call x1, Pallas kernels: 29.1 us -> 26.5 us  [body(): pl.pallas_call(functools.partial(kernel, (planes, fold, grp, heads)), out...]
    unnamed x1, local copies, waits for them, and re-layouts: 1.72 us -> 0.73 us
where the time goes in v1:
time: 27.5 us; the launch traced here: 27.3 us
  Pallas kernels  26.5 us (96%)
  local copies, waits for them, and re-layouts  0.73 us (3%)
    pallas_call x1, Pallas kernels, body(): pl.pallas_call(functools.partial(kernel, (planes, fold, grp, heads)), out...  26.5 us
    unnamed x1, local copies, waits for them, and re-layouts  0.73 us

profile of v1, /device:TPU:0, one launch (start us, length us, event | category | flops | bytes accessed | tf_op | source)
XLA Modules:
  0.0 27.3 jit_solution(3735960617921693875)
XLA Ops:
  0.0 26.5 %shard_map.46 = bf16[128,1280]{1,0:T(8,128)(2,1)S(1)} custom-call(s32[32]{0:T(128)} %img_hbm.1, bf16[128,1280]{1,0:T(8,128)(2,1)} %q_hbm.1, bf16[128,1280]{1,0:T(8,128)(2,1)} %k_hbm.1, bf16[128,1280]{1,0:T(8,128)(2,1)} %v_hbm.1), custom_call_target="tpu_custom_call" | custom-call | tf_op jit(solution)/shard_map/pallas_call | solution.py:320
  26.5 0.7 %copy.6 = bf16[128,1280]{1,0:T(8,128)(2,1)} copy(bf16[128,1280]{1,0:T(8,128)(2,1)S(1)} %shard_map.46) | data formatting | bytes 655360

commit v2 on v1

--- a/solution.py
+++ b/solution.py
@@ -87,23 +87,44 @@
     v_send, v_take, v_mate, v_sent = exchange(v_src, v_own, send_s.at[2], v_rs)
 
     def forward(which, halo, member, src):
+        pair = member // 2
+
         @pl.when(jnp.logical_and(has_next, member >= 1))
         def _():
-            remote(src, halo.at[member - 1], halo_ss.at[which, 0], halo_rs.at[which, 0],
+            remote(src, halo.at[member - 1], halo_ss.at[which, 0], halo_rs.at[which, 0, pair],
                    device(plane + 1, me)).start()
 
         @pl.when(jnp.logical_and(has_prev, member <= n - 2))
         def _():
-            remote(src, halo.at[n - 1 + member], halo_ss.at[which, 1], halo_rs.at[which, 1],
+            remote(src, halo.at[n - 1 + member], halo_ss.at[which, 1], halo_rs.at[which, 1, pair],
                    device(plane - 1, me)).start()
 
-    def take_below(which, halo):
-        part = halo.at[pl.ds(0, n - 1)]
-        remote(part, part, halo_ss.at[which, 0], halo_rs.at[which, 0], device(plane, mate)).wait_recv()
-
-    def take_above(which, halo):
-        part = halo.at[pl.ds(n - 1, n - 1)]
-        remote(part, part, halo_ss.at[which, 1], halo_rs.at[which, 1], device(plane, mate)).wait_recv()
+    def landed(which, halo, way, pair, first, count):
+        part = halo.at[pl.ds(first, count)]
+        remote(part, part, halo_ss.at[which, way], halo_rs.at[which, way, pair], device(plane, mate)).wait_recv()
+
+    def take_halo(which, halo, pair, use):
+        @pl.when(jnp.logical_and(has_prev, pair == 0))
+        def _():
+            landed(which, halo, 0, pair, 0, 1)
+            use(0, halo.at[0])
+
+        @pl.when(jnp.logical_and(has_prev, pair > 0))
+        def _():
+            landed(which, halo, 0, pair, 2 * pair - 1, 2)
+            for r in range(2):
+                use(2 * pair - 1 + r, halo.at[2 * pair - 1 + r])
+
+        @pl.when(jnp.logical_and(has_next, pair == pairs - 1))
+        def _():
+            landed(which, halo, 1, pair, 2 * n - 3, 1)
+            use(3 * n - 3, halo.at[2 * n - 3])
+
+        @pl.when(jnp.logical_and(has_next, pair < pairs - 1))
+        def _():
+            landed(which, halo, 1, pair, n - 1 + 2 * pair, 2)
+            for r in range(2):
+                use(2 * n - 1 + 2 * pair + r, halo.at[n - 1 + 2 * pair + r])
 
     def sent_up(which, halo):
         part = halo.at[pl.ds(0, n - 1)]
@@ -113,10 +134,22 @@
         part = halo.at[pl.ds(n - 1, n - 1)]
         remote(part, part, halo_ss.at[which, 1], halo_rs.at[which, 1], device(plane, mate)).wait_send()
 
+    across = grp // 2
+    fold_pair, grp_pair = mine // across, mine % across
+
+    def to_pair(step):
+        return (fold_pair + step // across) % fold * across + (grp_pair + step % across) % across
+
+    def from_pair(step):
+        return (fold_pair + fold - step // across) % fold * across + (grp_pair + across - step % across) % across
+
+    def arrival(turn):
+        return turn * across % (pairs - 1) + turn // (pairs - 1) * (pairs - 1)
+
     def out_order(send):
-        for step in range(1, pairs):
-            for r in range(2):
-                send((mine + pairs - step) % pairs * 2 + r)
+        for turn in range(1, pairs):
+            for r in (1, 0):
+                send(2 * to_pair(arrival(turn)) + r)
 
     loads[0].wait()
     turn(k_in, k_src)
@@ -132,7 +165,6 @@
     turn(q_in, q_src)
     q_send(mate)
     out_order(v_send)
-    out_order(q_send)
     keep = pltpu.make_async_copy(q_src.at[me], q_own.at[me], keep_s.at[0])
     keep.start()
     def natural(slot, src):
@@ -142,22 +174,23 @@
     vt[n - 1 + me] = v_src[me]
     k_mate()
     forward(0, k_halo, mate, k_own.at[mate])
-    natural(n - 1 + mate, k_own.at[mate])
-    def take_k(step, carry):
-        pair = (mine + step) % pairs
-        k_take(pair)
-        for r in range(2):
-            forward(0, k_halo, 2 * pair + r, k_own.at[2 * pair + r])
-        for r in range(2):
-            natural(n - 1 + 2 * pair + r, k_own.at[2 * pair + r])
-        return carry
-
-    lax.fori_loop(1, pairs, take_k, 0)
     v_mate()
     forward(1, v_halo, mate, v_own.at[mate])
+    natural(n - 1 + mate, k_own.at[mate])
     vt[n - 1 + mate] = v_own[mate]
+    def take_k(step, carry):
+        pair = from_pair(arrival(step))
+        k_take(pair)
+        for r in range(2):
+            forward(0, k_halo, 2 * pair + r, k_own.at[2 * pair + r])
+        for r in range(2):
+            natural(n - 1 + 2 * pair + r, k_own.at[2 * pair + r])
+        return carry
+
+    lax.fori_loop(1, pairs, take_k, 0)
+    out_order(q_send)
     def take_v(step, carry):
-        pair = (mine + step) % pairs
+        pair = from_pair(arrival(step))
         v_take(pair)
         for r in range(2):
             forward(1, v_halo, 2 * pair + r, v_own.at[2 * pair + r])
@@ -166,23 +199,11 @@
         return carry
 
     lax.fori_loop(1, pairs, take_v, 0)
-    def turn_below(i, carry):
-        natural(i, k_halo.at[i])
-        return carry
-
-    def turn_above(i, carry):
-        natural(n + i, k_halo.at[i])
-        return carry
-
-    @pl.when(has_prev)
-    def _():
-        take_below(0, k_halo)
-        lax.fori_loop(0, n - 1, turn_below, 0)
-
-    @pl.when(has_next)
-    def _():
-        take_above(0, k_halo)
-        lax.fori_loop(n - 1, 2 * n - 2, turn_above, 0)
+    def k_far(step, carry):
+        take_halo(0, k_halo, from_pair(arrival(step)), natural)
+        return carry
+
+    lax.fori_loop(0, pairs, k_far, 0)
     loads[3].wait()
     factor = math.log2(math.e) / math.sqrt(HDIM)
     blocks = img.shape[0]
@@ -228,11 +249,13 @@
             weights(2 * pair + r, r)
 
     def score_step(step, carry):
-        pair = (mine + step) % pairs
+        pair = from_pair(arrival(step))
+
         @pl.when(step == 0)
         def _():
             keep.wait()
             q_mate()
+
         @pl.when(step > 0)
         def _():
             q_take(pair)
@@ -240,27 +263,18 @@
         return carry
 
     lax.fori_loop(0, pairs, score_step, 0)
-    def move_below(i, carry):
-        vt[i] = v_halo[i]
-        return carry
-
-    def move_above(i, carry):
-        vt[n + i] = v_halo[i]
-        return carry
-
-    @pl.when(has_prev)
-    def _():
-        take_below(1, v_halo)
-        lax.fori_loop(0, n - 1, move_below, 0)
-
-    @pl.when(has_next)
-    def _():
-        take_above(1, v_halo)
-        lax.fori_loop(n - 1, 2 * n - 2, move_above, 0)
+    def hold(slot, src):
+        vt[slot] = src[...]
+
+    def v_far(step, carry):
+        take_halo(1, v_halo, from_pair(arrival(step)), hold)
+        return carry
+
+    lax.fori_loop(0, pairs, v_far, 0)
     o_send, o_take, o_mate, o_sent = exchange(o_src, o_own, send_s.at[3], o_rs)
 
     def finish(step, carry):
-        pair = (mine + 1 + step) % pairs
+        pair = to_pair(pairs - 1 - step)
         for r in range(2):
             m = 2 * pair + r
             start, _ = first_slot(m)
@@ -292,7 +306,7 @@
             sent_down(which, halo)
     o_mate()
     for step in range(1, pairs):
-        o_take((mine + step) % pairs)
+        o_take(from_pair(step))
     flat = jnp.concatenate([o_own[member] for member in range(n)], axis=0)
     for c in range(0, n * cols, BLK):
         out[:, c:c + BLK] = flat[c:c + BLK].T
@@ -330,7 +344,7 @@
                 pltpu.VMEM((2, MOST, BLK, lanes), f32),
                 pltpu.VMEM((n, MOST * BLK, lanes), bf),
                 slices, slices,
-            ] + [dma((4,))] + [dma((n // 2,))] * 4 + [dma((4,)), dma((2, 2)), dma((2, 2)), dma((1,))],
+            ] + [dma((4,))] + [dma((n // 2,))] * 4 + [dma((4,)), dma((2, 2)), dma((2, 2, n // 2)), dma((1,))],
             compiler_params=pltpu.CompilerParams(collective_id=0, has_side_effects=True,
                                                  vmem_limit_bytes=40 << 20),
         )(*args)

time: 27.5 us -> 26 us (0.945)
  Pallas kernels: 26.5 us -> 25.2 us
    pallas_call x1, Pallas kernels: 26.5 us -> 25.2 us  [body(): pl.pallas_call(functools.partial(kernel, (planes, fold, grp, heads)), out...]
where the time goes in v2:
time: 26 us; the launch traced here: 25.9 us
  Pallas kernels  25.2 us (97%)
  local copies, waits for them, and re-layouts  0.73 us (3%)
    pallas_call x1, Pallas kernels, body(): pl.pallas_call(functools.partial(kernel, (planes, fold, grp, heads)), out...  25.2 us
    unnamed x1, local copies, waits for them, and re-layouts  0.73 us

profile of v2, /device:TPU:0, one launch (start us, length us, event | category | flops | bytes accessed | tf_op | source)
XLA Modules:
  0.0 25.9 jit_solution(6314983433840741680)
XLA Ops:
  0.0 25.2 %shard_map.46 = bf16[128,1280]{1,0:T(8,128)(2,1)S(1)} custom-call(s32[32]{0:T(128)} %img_hbm.1, bf16[128,1280]{1,0:T(8,128)(2,1)} %q_hbm.1, bf16[128,1280]{1,0:T(8,128)(2,1)} %k_hbm.1, bf16[128,1280]{1,0:T(8,128)(2,1)} %v_hbm.1), custom_call_target="tpu_custom_call" | custom-call | tf_op jit(solution)/shard_map/pallas_call | solution.py:334
  25.2 0.7 %copy.6 = bf16[128,1280]{1,0:T(8,128)(2,1)} copy(bf16[128,1280]{1,0:T(8,128)(2,1)S(1)} %shard_map.46) | data formatting | bytes 655360

commit v3 on v2

--- a/solution.py
+++ b/solution.py
@@ -16,7 +16,7 @@
 
 
 def kernel(cfg, img_hbm, q_hbm, k_hbm, v_hbm, out, img, q_in, k_in, v_in, k_src, q_src, v_src,
-           k_own, q_own, v_own, k_halo, v_halo, kn, vt, l_scr, s_scr, p_scr, o_src, o_own,
+           k_own, q_own, v_own, k_halo, v_halo, kn, vt, l_scr, s_scr, p_scr, start_scr, count_scr, o_src, o_own,
            load_s, k_rs, q_rs, v_rs, o_rs, send_s, halo_ss, halo_rs, keep_s):
     planes, fold, grp, heads = cfg
     n = fold * grp
@@ -48,16 +48,6 @@
     @pl.when(has_next)
     def _():
         pl.semaphore_signal(barrier, inc=1, device_id=device(plane + 1, me), device_id_type=MESH)
-
-    @pl.when(jnp.logical_not(has_prev))
-    def _():
-        for ref in (kn, vt):
-            ref[0:n - 1] = jnp.zeros((n - 1,) + ref.shape[1:], ref.dtype)
-
-    @pl.when(jnp.logical_not(has_next))
-    def _():
-        for ref in (kn, vt):
-            ref[2 * n - 1:3 * n - 2] = jnp.zeros((n - 1,) + ref.shape[1:], ref.dtype)
     def turn(ref, dst):
         whole = jnp.concatenate([ref[:, c:c + BLK].T for c in range(0, n * cols, BLK)], axis=0)
         for member in range(n):
@@ -86,24 +76,29 @@
     q_send, q_take, q_mate, q_sent = exchange(q_src, q_own, send_s.at[1], q_rs)
     v_send, v_take, v_mate, v_sent = exchange(v_src, v_own, send_s.at[2], v_rs)
 
-    def forward(which, halo, member, src):
+    def forward(which, halo, member, src, down_first=False):
         pair = member // 2
 
-        @pl.when(jnp.logical_and(has_next, member >= 1))
-        def _():
-            remote(src, halo.at[member - 1], halo_ss.at[which, 0], halo_rs.at[which, 0, pair],
-                   device(plane + 1, me)).start()
-
-        @pl.when(jnp.logical_and(has_prev, member <= n - 2))
-        def _():
-            remote(src, halo.at[n - 1 + member], halo_ss.at[which, 1], halo_rs.at[which, 1, pair],
-                   device(plane - 1, me)).start()
+        def up():
+            @pl.when(jnp.logical_and(has_next, member >= 1))
+            def _():
+                remote(src, halo.at[member - 1], halo_ss.at[which, 0], halo_rs.at[which, 0, pair],
+                       device(plane + 1, me)).start()
+
+        def down():
+            @pl.when(jnp.logical_and(has_prev, member <= n - 2))
+            def _():
+                remote(src, halo.at[n - 1 + member], halo_ss.at[which, 1], halo_rs.at[which, 1, pair],
+                       device(plane - 1, me)).start()
+
+        for way in (down, up) if down_first else (up, down):
+            way()
 
     def landed(which, halo, way, pair, first, count):
         part = halo.at[pl.ds(first, count)]
         remote(part, part, halo_ss.at[which, way], halo_rs.at[which, way, pair], device(plane, mate)).wait_recv()
 
-    def take_halo(which, halo, pair, use):
+    def take_below(which, halo, pair, use):
         @pl.when(jnp.logical_and(has_prev, pair == 0))
         def _():
             landed(which, halo, 0, pair, 0, 1)
@@ -115,6 +110,7 @@
             for r in range(2):
                 use(2 * pair - 1 + r, halo.at[2 * pair - 1 + r])
 
+    def take_above(which, halo, pair, use):
         @pl.when(jnp.logical_and(has_next, pair == pairs - 1))
         def _():
             landed(which, halo, 1, pair, 2 * n - 3, 1)
@@ -145,6 +141,13 @@
 
     def arrival(turn):
         return turn * across % (pairs - 1) + turn // (pairs - 1) * (pairs - 1)
+
+    first_step = (fold - fold_pair) % fold * across + (across - grp_pair) % across
+
+    def turn_order(turn):
+        step = arrival(turn)
+        other = jnp.where(step == 1, pairs - 1, jnp.where(step == pairs - 1, 1, step))
+        return jnp.where(first_step == pairs - 1, other, step)
 
     def out_order(send):
         for turn in range(1, pairs):
@@ -159,7 +162,7 @@
     out_order(k_send)
     loads[2].wait()
     turn(v_in, v_src)
-    forward(1, v_halo, me, v_src.at[me])
+    forward(1, v_halo, me, v_src.at[me], True)
     v_send(mate)
     loads[1].wait()
     turn(q_in, q_src)
@@ -170,40 +173,6 @@
     def natural(slot, src):
         kn[slot] = src[...].T
 
-    natural(n - 1 + me, k_src.at[me])
-    vt[n - 1 + me] = v_src[me]
-    k_mate()
-    forward(0, k_halo, mate, k_own.at[mate])
-    v_mate()
-    forward(1, v_halo, mate, v_own.at[mate])
-    natural(n - 1 + mate, k_own.at[mate])
-    vt[n - 1 + mate] = v_own[mate]
-    def take_k(step, carry):
-        pair = from_pair(arrival(step))
-        k_take(pair)
-        for r in range(2):
-            forward(0, k_halo, 2 * pair + r, k_own.at[2 * pair + r])
-        for r in range(2):
-            natural(n - 1 + 2 * pair + r, k_own.at[2 * pair + r])
-        return carry
-
-    lax.fori_loop(1, pairs, take_k, 0)
-    out_order(q_send)
-    def take_v(step, carry):
-        pair = from_pair(arrival(step))
-        v_take(pair)
-        for r in range(2):
-            forward(1, v_halo, 2 * pair + r, v_own.at[2 * pair + r])
-        for r in range(2):
-            vt[n - 1 + 2 * pair + r] = v_own[2 * pair + r]
-        return carry
-
-    lax.fori_loop(1, pairs, take_v, 0)
-    def k_far(step, carry):
-        take_halo(0, k_halo, from_pair(arrival(step)), natural)
-        return carry
-
-    lax.fori_loop(0, pairs, k_far, 0)
     loads[3].wait()
     factor = math.log2(math.e) / math.sqrt(HDIM)
     blocks = img.shape[0]
@@ -219,66 +188,83 @@
             after += (high == own_id).astype(jnp.int32)
         return before, before + after + 1
 
-    def first_slot(m):
+    def note_span(m, carry):
         before, count = span(base + m)
-        return m + n - 1 - before, count
-
-    def weights(m, slot):
-        start, count = first_slot(m)
+        start_scr[m] = m + n - 1 - before
+        count_scr[m] = count
+        return carry
+
+    lax.fori_loop(0, n, note_span, 0)
+    natural(n - 1 + me, k_src.at[me])
+    vt[n - 1 + me] = v_src[me]
+    k_mate()
+    forward(0, k_halo, mate, k_own.at[mate])
+    v_mate()
+    forward(1, v_halo, mate, v_own.at[mate], True)
+    natural(n - 1 + mate, k_own.at[mate])
+    vt[n - 1 + mate] = v_own[mate]
+    def take_k(step, carry):
+        pair = from_pair(arrival(step))
+        k_take(pair)
+        for r in range(2):
+            forward(0, k_halo, 2 * pair + r, k_own.at[2 * pair + r], r == 1)
+        for r in range(2):
+            natural(n - 1 + 2 * pair + r, k_own.at[2 * pair + r])
+        return carry
+
+    lax.fori_loop(1, pairs, take_k, 0)
+    out_order(q_send)
+    def take_v(step, carry):
+        pair = from_pair(turn_order(step))
+        v_take(pair)
+        for r in range(2):
+            forward(1, v_halo, 2 * pair + r, v_own.at[2 * pair + r], r == 1)
+        for r in range(2):
+            vt[n - 1 + 2 * pair + r] = v_own[2 * pair + r]
+        return carry
+
+    lax.fori_loop(1, pairs, take_v, 0)
+    def k_far(step, carry):
+        take_below(0, k_halo, from_pair(arrival(step)), natural)
+        take_above(0, k_halo, from_pair(arrival(step)), natural)
+        return carry
+
+    lax.fori_loop(0, pairs, k_far, 0)
+    def scores(m, s_ref):
+        start, count = start_scr[m], count_scr[m]
         rows = []
         for h in range(heads):
             q_h = q_own[m, h * HDIM:(h + 1) * HDIM]
             none = jnp.zeros_like(q_h)
             rows.append(jnp.concatenate([q_h if j == h else none for j in range(heads)], axis=1))
         q_all = jnp.concatenate(rows, axis=0)
-        top = jnp.full((1, heads * BLK), NEG, jnp.float32)
+        top = jnp.full((8, heads * BLK), NEG, jnp.float32)
         for t in range(MOST):
-            s = jnp.dot(kn[start + t], q_all, preferred_element_type=jnp.float32)
-            s_scr[slot, t] = s
-            top = jnp.maximum(top, jnp.where(t < count, jnp.max(s, axis=0, keepdims=True), NEG))
+            s = jnp.dot(kn[start + jnp.where(t < count, t, 0)], q_all, preferred_element_type=jnp.float32)
+            s_ref[t] = s
+            high = jnp.max(s.reshape(BLK // 8, 8, heads * BLK), axis=0)
+            top = jnp.maximum(top, jnp.where(t < count, high, NEG))
+        return jnp.max(top, axis=0, keepdims=True), count
+
+    def weigh(m, s_ref, top, count):
         total = jnp.zeros((8, heads * BLK), jnp.float32)
         for t in range(MOST):
             shift = jnp.where(t < count, -top * factor, NEG)
-            w = jnp.exp2(s_scr[slot, t] * factor + shift)
+            w = jnp.exp2(s_ref[t] * factor + shift)
             total = total + jnp.sum(w.reshape(BLK // 8, 8, heads * BLK), axis=0)
             p_scr[m, t * BLK:(t + 1) * BLK] = w.astype(jnp.bfloat16)
         l_scr[m] = jnp.sum(total, axis=0, keepdims=True)
 
-    def score(pair):
-        for r in range(2):
-            weights(2 * pair + r, r)
-
-    def score_step(step, carry):
-        pair = from_pair(arrival(step))
-
-        @pl.when(step == 0)
-        def _():
-            keep.wait()
-            q_mate()
-
-        @pl.when(step > 0)
-        def _():
-            q_take(pair)
-        score(pair)
-        return carry
-
-    lax.fori_loop(0, pairs, score_step, 0)
     def hold(slot, src):
         vt[slot] = src[...]
 
-    def v_far(step, carry):
-        take_halo(1, v_halo, from_pair(arrival(step)), hold)
-        return carry
-
-    lax.fori_loop(0, pairs, v_far, 0)
     o_send, o_take, o_mate, o_sent = exchange(o_src, o_own, send_s.at[3], o_rs)
 
-    def finish(step, carry):
-        pair = to_pair(pairs - 1 - step)
+    def finish(pair):
         for r in range(2):
             m = 2 * pair + r
-            start, _ = first_slot(m)
-            v = jnp.concatenate([vt[start + t] for t in range(MOST)], axis=1)
+            start, count = start_scr[m], count_scr[m]
+            v = jnp.concatenate([vt[start + jnp.where(t < count, t, 0)] for t in range(MOST)], axis=1)
             res = jnp.dot(v, p_scr[m], preferred_element_type=jnp.float32)
             res = jnp.concatenate([res[h * HDIM:(h + 1) * HDIM, h * BLK:(h + 1) * BLK]
                                    / l_scr[m, :, h * BLK:(h + 1) * BLK] for h in range(heads)], axis=0)
@@ -289,9 +275,49 @@
             @pl.when(m != me)
             def _():
                 o_send(m)
-        return carry
-
-    lax.fori_loop(0, pairs, finish, 0)
+
+    keep.wait()
+    q_mate()
+    pair = from_pair(0)
+    now = scores(2 * pair, s_scr.at[0])
+    for step in range(pairs):
+        if step < pairs - 1:
+            coming = from_pair(turn_order(step + 1))
+            q_take(coming)
+        later = scores(2 * pair + 1, s_scr.at[1])
+        weigh(2 * pair, s_scr.at[0], *now)
+        if step < pairs - 1:
+            now = scores(2 * coming, s_scr.at[0])
+        weigh(2 * pair + 1, s_scr.at[1], *later)
+        pair = coming
+        if step == pairs - 2:
+            @pl.when(jnp.logical_not(has_prev))
+            def _():
+                take_above(1, v_halo, 0, hold)
+
+                @pl.when(mine != 0)
+                def _():
+                    finish(0)
+    @pl.when(has_prev)
+    def _():
+        for pair in range(pairs):
+            take_below(1, v_halo, pair, hold)
+        take_above(1, v_halo, 0, hold)
+
+        @pl.when(mine != 0)
+        def _():
+            finish(0)
+
+    def leave(pair, carry):
+        take_above(1, v_halo, pair, hold)
+
+        @pl.when(pair != mine)
+        def _():
+            finish(pair)
+        return carry
+
+    lax.fori_loop(1, pairs, leave, 0)
+    finish(mine)
     o_own[me] = o_src[me]
     k_sent()
     q_sent()
@@ -341,8 +367,9 @@
                 pltpu.VMEM((3 * n - 2, BLK, cols), bf),
                 pltpu.VMEM((3 * n - 2, cols, BLK), bf),
                 pltpu.VMEM((n, 1, lanes), f32),
-                pltpu.VMEM((2, MOST, BLK, lanes), f32),
+                pltpu.VMEM((4, MOST, BLK, lanes), f32),
                 pltpu.VMEM((n, MOST * BLK, lanes), bf),
+                pltpu.SMEM((n,), jnp.int32), pltpu.SMEM((n,), jnp.int32),
                 slices, slices,
             ] + [dma((4,))] + [dma((n // 2,))] * 4 + [dma((4,)), dma((2, 2)), dma((2, 2, n // 2)), dma((1,))],
             compiler_params=pltpu.CompilerParams(collective_id=0, has_side_effects=True,

time: 26 us -> 24.4 us (0.938)
  Pallas kernels: 25.2 us -> 23.5 us
    pallas_call x1, Pallas kernels: 25.2 us -> 23.5 us  [body(): pl.pallas_call(functools.partial(kernel, (planes, fold, grp, heads)), out...]
where the time goes in v3:
time: 24.4 us; the launch traced here: 24.3 us
  Pallas kernels  23.5 us (96%)
  local copies, waits for them, and re-layouts  0.73 us (3%)
    pallas_call x1, Pallas kernels, body(): pl.pallas_call(functools.partial(kernel, (planes, fold, grp, heads)), out...  23.5 us
    unnamed x1, local copies, waits for them, and re-layouts  0.73 us

profile of v3, /device:TPU:0, one launch (start us, length us, event | category | flops | bytes accessed | tf_op | source)
XLA Modules:
  0.0 24.3 jit_solution(321726058058921406)
XLA Ops:
  0.0 23.5 %shard_map.46 = bf16[128,1280]{1,0:T(8,128)(2,1)S(1)} custom-call(s32[32]{0:T(128)} %img_hbm.1, bf16[128,1280]{1,0:T(8,128)(2,1)} %q_hbm.1, bf16[128,1280]{1,0:T(8,128)(2,1)} %k_hbm.1, bf16[128,1280]{1,0:T(8,128)(2,1)} %v_hbm.1), custom_call_target="tpu_custom_call" | custom-call | tf_op jit(solution)/shard_map/pallas_call | solution.py:360
  23.6 0.7 %copy.6 = bf16[128,1280]{1,0:T(8,128)(2,1)} copy(bf16[128,1280]{1,0:T(8,128)(2,1)S(1)} %shard_map.46) | data formatting | bytes 655360

commit v4 on v3

--- a/solution.py
+++ b/solution.py
@@ -17,7 +17,7 @@
 
 def kernel(cfg, img_hbm, q_hbm, k_hbm, v_hbm, out, img, q_in, k_in, v_in, k_src, q_src, v_src,
            k_own, q_own, v_own, k_halo, v_halo, kn, vt, l_scr, s_scr, p_scr, start_scr, count_scr, o_src, o_own,
-           load_s, k_rs, q_rs, v_rs, o_rs, send_s, halo_ss, halo_rs, keep_s):
+           load_s, k_rs, q_rs, v_rs, o_rs, send_s, halo_ss, halo_rs):
     planes, fold, grp, heads = cfg
     n = fold * grp
     cols = heads * HDIM
@@ -59,22 +59,26 @@
 
     def exchange(src, dst, ss, rs):
         def send(to):
-            remote(src.at[to], dst.at[me], ss, rs.at[mine], device(plane, to)).start()
+            remote(src.at[to], dst.at[me], ss, rs.at[mine % rs.shape[0]], device(plane, to)).start()
 
         def take(pair):
             remote(src.at[pl.ds(0, 2)], dst.at[pl.ds(2 * pair, 2)], ss, rs.at[pair], device(plane, mate)).wait_recv()
 
         def take_mate():
             remote(src.at[0], dst.at[mate], ss, rs.at[mine], device(plane, mate)).wait_recv()
+
+        def take_all():
+            part = src.at[pl.ds(0, n - 1)]
+            remote(part, part, ss, rs.at[0], device(plane, mate)).wait_recv()
 
         def sent():
             part = src.at[pl.ds(0, n - 1)]
             remote(part, part, ss, rs.at[0], device(plane, mate)).wait_send()
-        return send, take, take_mate, sent
-
-    k_send, k_take, k_mate, k_sent = exchange(k_src, k_own, send_s.at[0], k_rs)
-    q_send, q_take, q_mate, q_sent = exchange(q_src, q_own, send_s.at[1], q_rs)
-    v_send, v_take, v_mate, v_sent = exchange(v_src, v_own, send_s.at[2], v_rs)
+        return send, take, take_mate, take_all, sent
+
+    k_send, k_take, k_mate, _, _ = exchange(k_src, k_own, send_s.at[0], k_rs)
+    q_send, q_take, q_mate, _, _ = exchange(q_src, q_own, send_s.at[0], q_rs)
+    v_send, v_take, v_mate, _, _ = exchange(v_src, v_own, send_s.at[0], v_rs)
 
     def forward(which, halo, member, src, down_first=False):
         pair = member // 2
@@ -93,6 +97,31 @@
 
         for way in (down, up) if down_first else (up, down):
             way()
+
+    def forward_pair(which, halo, pair, src):
+        def up(first, count):
+            remote(src.at[pl.ds(first, count)], halo.at[pl.ds(first - 1, count)], halo_ss.at[which, 0],
+                   halo_rs.at[which, 0, pair], device(plane + 1, me)).start()
+
+        def down(first, count):
+            remote(src.at[pl.ds(first, count)], halo.at[pl.ds(n - 1 + first, count)], halo_ss.at[which, 1],
+                   halo_rs.at[which, 1, pair], device(plane - 1, me)).start()
+
+        @pl.when(jnp.logical_and(has_next, pair > 0))
+        def _():
+            up(2 * pair, 2)
+
+        @pl.when(jnp.logical_and(has_next, pair == 0))
+        def _():
+            up(1, 1)
+
+        @pl.when(jnp.logical_and(has_prev, pair < pairs - 1))
+        def _():
+            down(2 * pair, 2)
+
+        @pl.when(jnp.logical_and(has_prev, pair == pairs - 1))
+        def _():
+            down(n - 2, 1)
 
     def landed(which, halo, way, pair, first, count):
         part = halo.at[pl.ds(first, count)]
@@ -168,8 +197,6 @@
     turn(q_in, q_src)
     q_send(mate)
     out_order(v_send)
-    keep = pltpu.make_async_copy(q_src.at[me], q_own.at[me], keep_s.at[0])
-    keep.start()
     def natural(slot, src):
         kn[slot] = src[...].T
 
@@ -206,8 +233,7 @@
     def take_k(step, carry):
         pair = from_pair(arrival(step))
         k_take(pair)
-        for r in range(2):
-            forward(0, k_halo, 2 * pair + r, k_own.at[2 * pair + r], r == 1)
+        forward_pair(0, k_halo, pair, k_own)
         for r in range(2):
             natural(n - 1 + 2 * pair + r, k_own.at[2 * pair + r])
         return carry
@@ -217,8 +243,7 @@
     def take_v(step, carry):
         pair = from_pair(turn_order(step))
         v_take(pair)
-        for r in range(2):
-            forward(1, v_halo, 2 * pair + r, v_own.at[2 * pair + r], r == 1)
+        forward_pair(1, v_halo, pair, v_own)
         for r in range(2):
             vt[n - 1 + 2 * pair + r] = v_own[2 * pair + r]
         return carry
@@ -258,7 +283,7 @@
     def hold(slot, src):
         vt[slot] = src[...]
 
-    o_send, o_take, o_mate, o_sent = exchange(o_src, o_own, send_s.at[3], o_rs)
+    o_send, _, _, o_take, o_sent = exchange(o_src, o_own, send_s.at[1], o_rs)
 
     def finish(pair):
         for r in range(2):
@@ -276,7 +301,7 @@
             def _():
                 o_send(m)
 
-    keep.wait()
+    q_own[me] = q_src[me]
     q_mate()
     pair = from_pair(0)
     now = scores(2 * pair, s_scr.at[0])
@@ -319,9 +344,8 @@
     lax.fori_loop(1, pairs, leave, 0)
     finish(mine)
     o_own[me] = o_src[me]
-    k_sent()
-    q_sent()
-    v_sent()
+    part = vt.at[pl.ds(0, 3 * n - 3)]
+    remote(part, part, send_s.at[0], k_rs.at[0], device(plane, mate)).wait_send()
     for which, halo in ((0, k_halo), (1, v_halo)):
         @pl.when(has_next)
         def _():
@@ -330,9 +354,7 @@
         @pl.when(has_prev)
         def _():
             sent_down(which, halo)
-    o_mate()
-    for step in range(1, pairs):
-        o_take(from_pair(step))
+    o_take()
     flat = jnp.concatenate([o_own[member] for member in range(n)], axis=0)
     for c in range(0, n * cols, BLK):
         out[:, c:c + BLK] = flat[c:c + BLK].T
@@ -371,7 +393,7 @@
                 pltpu.VMEM((n, MOST * BLK, lanes), bf),
                 pltpu.SMEM((n,), jnp.int32), pltpu.SMEM((n,), jnp.int32),
                 slices, slices,
-            ] + [dma((4,))] + [dma((n // 2,))] * 4 + [dma((4,)), dma((2, 2)), dma((2, 2, n // 2)), dma((1,))],
+            ] + [dma((4,))] + [dma((n // 2,))] * 3 + [dma((1,)), dma((2,)), dma((2, 2)), dma((2, 2, n // 2))],
             compiler_params=pltpu.CompilerParams(collective_id=0, has_side_effects=True,
                                                  vmem_limit_bytes=40 << 20),
         )(*args)

time: 24.4 us -> 24.4 us (level)
  no operation moved by 1% of the time
where the time goes in v4:
time: 24.4 us; the launch traced here: 24.2 us
  Pallas kernels  23.5 us (96%)
  local copies, waits for them, and re-layouts  0.73 us (3%)
    pallas_call x1, Pallas kernels, body(): pl.pallas_call(functools.partial(kernel, (planes, fold, grp, heads)), out...  23.5 us
    unnamed x1, local copies, waits for them, and re-layouts  0.73 us

profile of v4, /device:TPU:0, one launch (start us, length us, event | category | flops | bytes accessed | tf_op | source)
XLA Modules:
  0.0 24.2 jit_solution(18101381734998174168)
XLA Ops:
  0.0 23.5 %shard_map.46 = bf16[128,1280]{1,0:T(8,128)(2,1)S(1)} custom-call(s32[32]{0:T(128)} %img_hbm.1, bf16[128,1280]{1,0:T(8,128)(2,1)} %q_hbm.1, bf16[128,1280]{1,0:T(8,128)(2,1)} %k_hbm.1, bf16[128,1280]{1,0:T(8,128)(2,1)} %v_hbm.1), custom_call_target="tpu_custom_call" | custom-call | tf_op jit(solution)/shard_map/pallas_call | solution.py:382
  23.5 0.7 %copy.6 = bf16[128,1280]{1,0:T(8,128)(2,1)} copy(bf16[128,1280]{1,0:T(8,128)(2,1)S(1)} %shard_map.46) | data formatting | bytes 655360

commit v5 on v4

--- a/solution.py
+++ b/solution.py
@@ -285,7 +285,7 @@
 
     o_send, _, _, o_take, o_sent = exchange(o_src, o_own, send_s.at[1], o_rs)
 
-    def finish(pair):
+    def finish(pair, local=False, lead=0):
         for r in range(2):
             m = 2 * pair + r
             start, count = start_scr[m], count_scr[m]
@@ -294,12 +294,9 @@
             res = jnp.concatenate([res[h * HDIM:(h + 1) * HDIM, h * BLK:(h + 1) * BLK]
                                    / l_scr[m, :, h * BLK:(h + 1) * BLK] for h in range(heads)], axis=0)
             o_src[m] = res.astype(jnp.bfloat16)
-        for r in range(2):
-            m = 2 * pair + r
-
-            @pl.when(m != me)
-            def _():
-                o_send(m)
+        if not local:
+            for r in range(2):
+                o_send(2 * pair + (lead + r) % 2)
 
     q_own[me] = q_src[me]
     q_mate()
@@ -331,18 +328,19 @@
 
         @pl.when(mine != 0)
         def _():
-            finish(0)
+            finish(0, lead=0)
 
     def leave(pair, carry):
         take_above(1, v_halo, pair, hold)
 
         @pl.when(pair != mine)
         def _():
-            finish(pair)
+            finish(pair, lead=me)
         return carry
 
     lax.fori_loop(1, pairs, leave, 0)
-    finish(mine)
+    finish(mine, True)
+    o_send(mate)
     o_own[me] = o_src[me]
     part = vt.at[pl.ds(0, 3 * n - 3)]
     remote(part, part, send_s.at[0], k_rs.at[0], device(plane, mate)).wait_send()

time: 24.4 us -> 24.4 us (level)
  no operation moved by 1% of the time
where the time goes in v5:
time: 24.4 us; the launch traced here: 24.2 us
  Pallas kernels  23.5 us (96%)
  local copies, waits for them, and re-layouts  0.73 us (3%)
    pallas_call x1, Pallas kernels, body(): pl.pallas_call(functools.partial(kernel, (planes, fold, grp, heads)), out...  23.5 us
    unnamed x1, local copies, waits for them, and re-layouts  0.73 us

profile of v5, /device:TPU:0, one launch (start us, length us, event | category | flops | bytes accessed | tf_op | source)
XLA Modules:
  0.0 24.2 jit_solution(11949186420407778934)
XLA Ops:
  0.0 23.5 %shard_map.46 = bf16[128,1280]{1,0:T(8,128)(2,1)S(1)} custom-call(s32[32]{0:T(128)} %img_hbm.1, bf16[128,1280]{1,0:T(8,128)(2,1)} %q_hbm.1, bf16[128,1280]{1,0:T(8,128)(2,1)} %k_hbm.1, bf16[128,1280]{1,0:T(8,128)(2,1)} %v_hbm.1), custom_call_target="tpu_custom_call" | custom-call | tf_op jit(solution)/shard_map/pallas_call | solution.py:380
  23.5 0.7 %copy.6 = bf16[128,1280]{1,0:T(8,128)(2,1)} copy(bf16[128,1280]{1,0:T(8,128)(2,1)S(1)} %shard_map.46) | data formatting | bytes 655360

commit v6 on v5

--- a/solution.py
+++ b/solution.py
@@ -31,7 +31,7 @@
     has_prev, has_next = plane > 0, plane < planes - 1
 
     loads = [pltpu.make_async_copy(src, dst, load_s.at[i])
-             for i, (src, dst) in enumerate(((k_hbm, k_in), (q_hbm, q_in), (v_hbm, v_in), (img_hbm, img)))]
+             for i, (src, dst) in enumerate(((k_hbm, k_in), (v_hbm, v_in), (q_hbm, q_in), (img_hbm, img)))]
     for load in loads:
         load.start()
     def device(at_plane, member):
@@ -189,11 +189,11 @@
     forward(0, k_halo, me, k_src.at[me])
     k_send(mate)
     out_order(k_send)
-    loads[2].wait()
+    loads[1].wait()
     turn(v_in, v_src)
     forward(1, v_halo, me, v_src.at[me], True)
     v_send(mate)
-    loads[1].wait()
+    loads[2].wait()
     turn(q_in, q_src)
     q_send(mate)
     out_order(v_send)
@@ -283,7 +283,13 @@
     def hold(slot, src):
         vt[slot] = src[...]
 
-    o_send, _, _, o_take, o_sent = exchange(o_src, o_own, send_s.at[1], o_rs)
+    _, _, _, _, o_sent = exchange(o_src, o_own, send_s.at[1], o_rs)
+
+    def o_send(to):
+        away = (to // grp + fold - fold_at) % fold
+        remote(o_src.at[to], o_own.at[me], send_s.at[1], o_rs.at[(away + fold - 1) // fold],
+               device(plane, to)).start()
+
 
     def finish(pair, local=False, lead=0):
         for r in range(2):
@@ -352,10 +358,20 @@
         @pl.when(has_prev)
         def _():
             sent_down(which, halo)
-    o_take()
-    flat = jnp.concatenate([o_own[member] for member in range(n)], axis=0)
-    for c in range(0, n * cols, BLK):
-        out[:, c:c + BLK] = flat[c:c + BLK].T
+    half = n // fold
+    width = half * cols
+
+    def settle(which, count):
+        part = o_own.at[pl.ds(0, count)]
+        remote(part, part, send_s.at[1], o_rs.at[which], device(plane, mate)).wait_recv()
+        for f in range(1, fold) if which else range(1):
+            at = (fold_at + f) % fold
+            flat = jnp.concatenate([o_own[at * half + i] for i in range(half)], axis=0)
+            for c in range(0, width, BLK):
+                out[:, pl.ds(pl.multiple_of(at * width + c, BLK), BLK)] = flat[c:c + BLK].T
+
+    settle(0, half - 1)
+    settle(1, n - half)
     o_sent()
 
 
@@ -391,7 +407,7 @@
                 pltpu.VMEM((n, MOST * BLK, lanes), bf),
                 pltpu.SMEM((n,), jnp.int32), pltpu.SMEM((n,), jnp.int32),
                 slices, slices,
-            ] + [dma((4,))] + [dma((n // 2,))] * 3 + [dma((1,)), dma((2,)), dma((2, 2)), dma((2, 2, n // 2))],
+            ] + [dma((4,))] + [dma((n // 2,))] * 3 + [dma((2,)), dma((2,)), dma((2, 2)), dma((2, 2, n // 2))],
             compiler_params=pltpu.CompilerParams(collective_id=0, has_side_effects=True,
                                                  vmem_limit_bytes=40 << 20),
         )(*args)

time: 24.4 us -> 24.4 us (level)
  no operation moved by 1% of the time
where the time goes in v6:
time: 24.4 us; the launch traced here: 24.2 us
  Pallas kernels  23.5 us (96%)
  local copies, waits for them, and re-layouts  0.73 us (3%)
    pallas_call x1, Pallas kernels, body(): pl.pallas_call(functools.partial(kernel, (planes, fold, grp, heads)), out...  23.5 us
    unnamed x1, local copies, waits for them, and re-layouts  0.73 us

profile of v6, /device:TPU:0, one launch (start us, length us, event | category | flops | bytes accessed | tf_op | source)
XLA Modules:
  0.0 24.2 jit_solution(14959486115160468884)
XLA Ops:
  0.0 23.5 %shard_map.46 = bf16[128,1280]{1,0:T(8,128)(2,1)S(1)} custom-call(s32[32]{0:T(128)} %img_hbm.1, bf16[128,1280]{1,0:T(8,128)(2,1)} %q_hbm.1, bf16[128,1280]{1,0:T(8,128)(2,1)} %k_hbm.1, bf16[128,1280]{1,0:T(8,128)(2,1)} %v_hbm.1), custom_call_target="tpu_custom_call" | custom-call | tf_op jit(solution)/shard_map/pallas_call | solution.py:396
  23.5 0.7 %copy.6 = bf16[128,1280]{1,0:T(8,128)(2,1)} copy(bf16[128,1280]{1,0:T(8,128)(2,1)S(1)} %shard_map.46) | data formatting | bytes 655360

commit v7 on v6

--- a/solution.py
+++ b/solution.py
@@ -178,9 +178,9 @@
         other = jnp.where(step == 1, pairs - 1, jnp.where(step == pairs - 1, 1, step))
         return jnp.where(first_step == pairs - 1, other, step)
 
-    def out_order(send):
+    def out_order(send, cores=(1, 0)):
         for turn in range(1, pairs):
-            for r in (1, 0):
+            for r in cores:
                 send(2 * to_pair(arrival(turn)) + r)
 
     loads[0].wait()
@@ -239,7 +239,8 @@
         return carry
 
     lax.fori_loop(1, pairs, take_k, 0)
-    out_order(q_send)
+    out_order(q_send, (1,))
+    out_order(q_send, (0,))
     def take_v(step, carry):
         pair = from_pair(turn_order(step))
         v_take(pair)

time: 24.4 us -> 24.3 us (level)
  no operation moved by 1% of the time
where the time goes in v7:
time: 24.3 us; the launch traced here: 24.2 us
  Pallas kernels  23.5 us (97%)
  local copies, waits for them, and re-layouts  0.73 us (3%)
    pallas_call x1, Pallas kernels, body(): pl.pallas_call(functools.partial(kernel, (planes, fold, grp, heads)), out...  23.5 us
    unnamed x1, local copies, waits for them, and re-layouts  0.73 us

profile of v7, /device:TPU:0, one launch (start us, length us, event | category | flops | bytes accessed | tf_op | source)
XLA Modules:
  0.0 24.2 jit_solution(2282812817986079685)
XLA Ops:
  0.0 23.5 %shard_map.46 = bf16[128,1280]{1,0:T(8,128)(2,1)S(1)} custom-call(s32[32]{0:T(128)} %img_hbm.1, bf16[128,1280]{1,0:T(8,128)(2,1)} %q_hbm.1, bf16[128,1280]{1,0:T(8,128)(2,1)} %k_hbm.1, bf16[128,1280]{1,0:T(8,128)(2,1)} %v_hbm.1), custom_call_target="tpu_custom_call" | custom-call | tf_op jit(solution)/shard_map/pallas_call | solution.py:397
  23.5 0.7 %copy.6 = bf16[128,1280]{1,0:T(8,128)(2,1)} copy(bf16[128,1280]{1,0:T(8,128)(2,1)S(1)} %shard_map.46) | data formatting | bytes 655360

commit v8 on v6

--- a/solution.py
+++ b/solution.py
@@ -187,8 +187,8 @@
     turn(k_in, k_src)
     pl.semaphore_wait(barrier, n - 1 + has_prev.astype(jnp.int32) + has_next.astype(jnp.int32))
     forward(0, k_halo, me, k_src.at[me])
+    out_order(k_send)
     k_send(mate)
-    out_order(k_send)
     loads[1].wait()
     turn(v_in, v_src)
     forward(1, v_halo, me, v_src.at[me], True)

time: 24.4 us -> 24.4 us (level)
  no operation moved by 1% of the time
where the time goes in v8:
time: 24.4 us; the launch traced here: 24.2 us
  Pallas kernels  23.5 us (96%)
  local copies, waits for them, and re-layouts  0.73 us (3%)
    pallas_call x1, Pallas kernels, body(): pl.pallas_call(functools.partial(kernel, (planes, fold, grp, heads)), out...  23.5 us
    unnamed x1, local copies, waits for them, and re-layouts  0.73 us

profile of v8, /device:TPU:0, one launch (start us, length us, event | category | flops | bytes accessed | tf_op | source)
XLA Modules:
  0.0 24.2 jit_solution(14955344958200119188)
XLA Ops:
  0.0 23.5 %shard_map.46 = bf16[128,1280]{1,0:T(8,128)(2,1)S(1)} custom-call(s32[32]{0:T(128)} %img_hbm.1, bf16[128,1280]{1,0:T(8,128)(2,1)} %q_hbm.1, bf16[128,1280]{1,0:T(8,128)(2,1)} %k_hbm.1, bf16[128,1280]{1,0:T(8,128)(2,1)} %v_hbm.1), custom_call_target="tpu_custom_call" | custom-call | tf_op jit(solution)/shard_map/pallas_call | solution.py:396
  23.5 0.7 %copy.6 = bf16[128,1280]{1,0:T(8,128)(2,1)} copy(bf16[128,1280]{1,0:T(8,128)(2,1)S(1)} %shard_map.46) | data formatting | bytes 655360
